TPU v7x, 32 devices: a whole 2x2x4 slice. The times are simulated.
32 devices in a mesh: space: 4 (over z), vel: 8 (over y, x, core).
Axes of the slice: x: 2, y: 2, z: 4, core: 2. Of those that a mesh axis runs over, the one named last changes fastest.
Arguments:
- dist: float32 [64, 16, 16, 2048], P('space', None, None, 'vel'), may hold values from 0.05 to 2
- relax_rate: float32 [64, 16, 16], P('space'), may hold values from 0.2 to 0.9
- kinetic_cells: int32 [2, 16384], P(None, 'space'), may hold values from 0 to 4095, as said below
- kinetic_count: int32 [2, 4], replicated, may hold values from 1 to 4096, 8192 in all within a row
- map_a: bfloat16 [2048, 768], replicated, may hold values from -0.125 to 0.125
- map_b: bfloat16 [2048, 768], replicated, may hold values from -0.125 to 0.125
- map_c: bfloat16 [768, 2048], replicated, may hold values from -0.21875 to 0.21875
Outputs:
- dist_out: float32 [64, 16, 16, 2048], P('space', None, None, 'vel')
Inputs may be any that keep to these rules, and one draw needn't show every extreme that they name: `kinetic_cells`: for each step, the 4096 entries of a slab's block are a permutation of that slab's local cell numbers. `kinetic_count`: each step's counts sum to 8192, and one slab is kinetic in all its cells.
All inputs are finite; a program needn't handle non-finite values.
Results may differ from a plain program's by a relative error of at most 0.0034.
Values may be sent and summed in bfloat16 or wider, within the bound.
A program may use at most 128 MiB of HBM per device.

v0:
```python
import functools
import math

import jax
import jax.numpy as jnp
import numpy as np
from jax import lax
from jax.experimental import pallas as pl
from jax.experimental.pallas import tpu as pltpu
from jax.sharding import PartitionSpec as P

GX = 16
GY = 16
GZ = 8
STEPS = 2
COURANT = 0.1
SPACING = 0.5
COLLIDE = 0.5
LANES = 128
CHUNKS = 8
MESH = pl.DeviceIdType.MESH


def tables():
    k = np.arange(GX * GY * GZ)
    vx = ((k // (GY * GZ)) - 0.5 * (GX - 1)) * SPACING
    vy = (((k // GZ) % GY) - 0.5 * (GY - 1)) * SPACING
    vz = ((k % GZ) - 0.5 * (GZ - 1)) * SPACING
    s = vx * vx + vy * vy + vz * vz
    w = np.exp(-0.5 * s)
    w = w / w.sum()
    m2, m4 = (w * s).sum(), (w * s * s).sum()
    kappa = m4 - m2 * m2
    per_e = w * (s - m2) / kappa
    rows = np.stack([
        w - m2 * per_e,
        w * vx / (w * vx * vx).sum(),
        w * vy / (w * vy * vy).sum(),
        w * vz / (w * vz * vz).sum(),
        per_e,
        per_e,
    ])
    s_hi = np.asarray(np.asarray(s, np.float32).astype(jnp.bfloat16), np.float64)
    cols = np.stack([np.ones_like(vx), vx, vy, vz, s_hi, s - s_hi], axis=1)
    g_hi = np.asarray(np.asarray(rows, np.float32).astype(jnp.bfloat16), np.float64)
    g_lo = rows - g_hi
    basis = np.zeros((24, k.size))
    back = np.zeros((24, k.size))
    for at, part in ((0, g_hi), (8, g_hi), (16, g_lo)):
        basis[at:at + 6] = cols.T
        back[at:at + 6] = part
    return basis.astype(np.float32), back.astype(np.float32)


def limited(a, b):
    return jnp.minimum(jnp.maximum(a, jnp.minimum(b, 0.0)), jnp.maximum(b, 0.0))


def merged(code_row, moved, payload, own_back):
    code = jnp.broadcast_to(code_row, (LANES, LANES)).T
    equilibrium = jnp.dot(payload[:, :LANES], own_back, preferred_element_type=jnp.float32)
    out = []
    for t in range(moved.shape[1] // LANES):
        cols = slice(t * LANES, (t + 1) * LANES)
        old = moved[:, cols]
        fluid = old + code * (equilibrium[:, cols] - old)
        out.append(jnp.where(code < 0.0, old - code * payload[:, cols].astype(jnp.float32), fluid))
    return jnp.concatenate(out, axis=1)


def kernel(dims, counts, kin_cells, relax, basis_rows, back, dist, a_hbm, b_hbm, c_hbm,
           moved_out, ret_out, codes,
           cur, moved, cprev, halo, sendbuf, recv, res, ret, map_a, map_b, map_c, basis, spread,
           load_sem, const_sem, local_sem, out_sem, halo_send, halo_recv, row_send, row_recv, res_send, res_recv):
    nx, ny, nz, width, groups, slabs = dims
    plane = ny * nz
    cells = nx * plane
    chunk = cells // CHUNKS
    rows = chunk // groups
    planes = nx // CHUNKS
    tiles = width // LANES
    me = lax.axis_index("vel")
    slab = lax.axis_index("space")
    first_x = (me * width) // (GY * GZ)
    bit = first_x // (GX // 2)
    sign = 2 * bit - 1
    ahead = lax.rem(slab + sign + slabs, slabs)
    behind = lax.rem(slab - sign + slabs, slabs)

    pieces = [0, CHUNKS - 1] + list(range(1, CHUNKS - 1))
    loads = {}
    for c in pieces:
        loads[c] = pltpu.make_async_copy(
            dist.at[pl.ds(c * chunk, chunk)], cur.at[pl.ds(2 * plane + c * chunk, chunk)], load_sem.at[c])
        loads[c].start()
    consts = []
    for n, (src, dst) in enumerate(((a_hbm, map_a), (b_hbm, map_b), (c_hbm, map_c))):
        consts.append(pltpu.make_async_copy(src, dst, const_sem.at[n]))
        consts[-1].start()

    barrier = pltpu.get_barrier_semaphore()
    for p in range(1, groups):
        pl.semaphore_signal(barrier, inc=1, device_id={"vel": lax.rem(me + p, groups)}, device_id_type=MESH)
    pl.semaphore_signal(barrier, inc=1, device_id={"space": ahead}, device_id_type=MESH)
    pl.semaphore_signal(barrier, inc=1, device_id={"space": behind}, device_id_type=MESH)
    pl.semaphore_wait(barrier, groups + 1)

    @pl.loop(0, basis.shape[0] // LANES)
    def _(n):
        here = pl.ds(pl.multiple_of(n * LANES, LANES), LANES)
        part = basis_rows[:, here]
        whole = jnp.concatenate([part, jnp.zeros((LANES - part.shape[0], LANES), jnp.float32)], axis=0)
        basis[here] = whole.T.astype(jnp.bfloat16)

    groups_of = cells // LANES
    span = 4 * LANES
    for step in range(STEPS):
        count = counts[step, slab]
        flags = jnp.zeros((groups_of, LANES), jnp.float32)
        for n in range(cells // span):
            which = kin_cells[step:step + 1, n * span:(n + 1) * span]
            live = n * span + lax.broadcasted_iota(jnp.int32, (1, span), 1) < count
            quotient = jnp.where(live, lax.div(which, LANES), -1)
            hot_high = lax.broadcasted_iota(jnp.int32, (groups_of, span), 0) == quotient
            hot_low = lax.broadcasted_iota(jnp.int32, (LANES, span), 0) == lax.rem(which, LANES)
            flags += lax.dot_general(
                jnp.where(hot_high, 1.0, 0.0).astype(jnp.bfloat16), jnp.where(hot_low, 1.0, 0.0).astype(jnp.bfloat16),
                (((1,), (1,)), ((), ())), preferred_element_type=jnp.float32)
        codes[step] = jnp.where(flags > 0.5, -COLLIDE, relax[...])

    lane = lax.broadcasted_iota(jnp.int32, (1, LANES), 1)
    vy = (((lane // GZ) % GY).astype(jnp.float32) - 0.5 * (GY - 1)) * SPACING
    vz = ((lane % GZ).astype(jnp.float32) - 0.5 * (GZ - 1)) * SPACING
    block = (nz, LANES)
    pos_y = jnp.broadcast_to(vy > 0.0, block)
    pos_z = jnp.broadcast_to(vz > 0.0, block)
    half_y = jnp.broadcast_to(jnp.where(vy > 0.0, 0.5, -0.5), block)
    half_z = jnp.broadcast_to(jnp.where(vz > 0.0, 0.5, -0.5), block)
    rate_y = jnp.broadcast_to(COURANT * jnp.abs(vy), block)
    rate_z = jnp.broadcast_to(COURANT * jnp.abs(vz), block)

    def pick(positive, negative):
        return bit * positive + (1 - bit) * negative

    def at(index, y):
        return pl.ds(pl.multiple_of(index * plane + y * nz, nz), nz)

    def x_state(index, y, cols):
        mid = cur[at(index, y), cols]
        slope = limited(mid - cur[at(index - sign, y), cols], cur[at(index + sign, y), cols] - mid)
        return mid + 0.5 * slope

    def transport(c):
        start = pick(2 + c * planes, 2 + (c + 1) * planes - 1)

        @pl.loop(0, ny)
        def _(y):
            for t in range(tiles):
                cols = pl.ds(t * LANES, LANES)
                cprev[pl.ds(pl.multiple_of(y * nz, nz), nz), cols] = x_state(start - sign, y, cols)

        @pl.loop(0, planes)
        def _(j):
            index = start + sign * j
            @pl.loop(0, tiles)
            def _(t):
                cols = pl.ds(pl.multiple_of(t * LANES, LANES), LANES)
                vx = (((me * width + t * LANES) // (GY * GZ)).astype(jnp.float32) - 0.5 * (GX - 1)) * SPACING
                rate_x = COURANT * jnp.abs(vx)

                def value(y):
                    return cur[at(index, y % ny), cols]

                def y_state(mid, before, after):
                    return mid + half_y * limited(before, after)

                f = {y: value(y) for y in range(-2, 2)}
                d = {y: f[y + 1] - f[y] for y in (-2, -1, 0)}
                cy = {y: y_state(f[y], d[y - 1], d[y]) for y in (-1, 0)}
                for y in range(ny):
                    f[y + 2] = value(y + 2)
                    d[y + 1] = f[y + 2] - f[y + 1]
                    cy[y + 1] = y_state(f[y + 1], d[y], d[y + 1])
                    mid = f[y]
                    total = rate_y * (cy[y] - jnp.where(pos_y, cy[y - 1], cy[y + 1]))
                    dz = pltpu.roll(mid, nz - 1, 0) - mid
                    cz = mid + half_z * limited(pltpu.roll(dz, 1, 0), dz)
                    total += rate_z * (cz - jnp.where(pos_z, pltpu.roll(cz, 1, 0), pltpu.roll(cz, nz - 1, 0)))
                    cx = x_state(index, y, cols)
                    here = pl.ds(y * nz, nz)
                    total += rate_x * (cx - cprev[here, cols])
                    cprev[here, cols] = cx
                    result = mid - total
                    moved[at(index - 2, y), cols] = result
                    sendbuf[at(index - 2, y), cols] = result.astype(jnp.bfloat16)

    def row_copies(c):
        out = []
        for p in range(1, groups):
            peer = lax.rem(me + p, groups)
            out.append(pltpu.make_async_remote_copy(
                src_ref=sendbuf.at[pl.ds(pl.multiple_of(c * chunk + peer * rows, rows), rows)],
                dst_ref=recv.at[me, pl.ds(c * rows, rows)],
                send_sem=row_send.at[c, p], recv_sem=row_recv.at[c, p],
                device_id={"vel": peer}, device_id_type=MESH))
        return out

    def row_local(c):
        return pltpu.make_async_copy(
            sendbuf.at[pl.ds(pl.multiple_of(c * chunk + me * rows, rows), rows)],
            recv.at[me, pl.ds(c * rows, rows)], local_sem.at[0, c])

    def res_copies(c):
        out = []
        for p in range(1, groups):
            peer = lax.rem(me + p, groups)
            out.append(pltpu.make_async_remote_copy(
                src_ref=res.at[peer, pl.ds(c * rows, rows)],
                dst_ref=ret.at[pl.ds(pl.multiple_of(c * chunk + me * rows, rows), rows)],
                send_sem=res_send.at[c, p], recv_sem=res_recv.at[c, p],
                device_id={"vel": peer}, device_id_type=MESH))
        return out

    def res_local(c):
        return pltpu.make_async_copy(
            res.at[me, pl.ds(c * rows, rows)],
            ret.at[pl.ds(pl.multiple_of(c * chunk + me * rows, rows), rows)], local_sem.at[1, c])

    def collide(step, c):
        here = pl.ds(c * rows, rows)
        first = second = mom = None
        for s in range(groups):
            part = recv[s, here]
            cols = pl.ds(s * width, width)
            terms = [jnp.dot(part, m[cols], preferred_element_type=jnp.float32) for m in (map_a, map_b, basis)]
            first, second, mom = terms if s == 0 else [old + new for old, new in zip((first, second, mom), terms)]
        hidden = (first * second).astype(jnp.bfloat16)
        high = mom.astype(jnp.bfloat16).astype(jnp.float32)
        is_low = (lax.broadcasted_iota(jnp.int32, mom.shape, 1) // 8) == 1
        split = jnp.where(is_low, mom - high, high)
        begin = c * chunk + me * rows
        spread[...] = jnp.broadcast_to(codes[step, pl.ds(begin // LANES, 1)], (LANES, LANES)).T
        kin = spread[pl.ds(pl.multiple_of(lax.rem(begin, LANES), math.gcd(rows, LANES)), rows)] < 0.0
        for s in range(groups):
            cols = pl.ds(s * width, width)
            out = jnp.dot(hidden, map_c[:, cols], preferred_element_type=jnp.float32)
            res[s, here, :LANES] = jnp.where(kin, out[:, :LANES], split).astype(jnp.bfloat16)
            if tiles > 1:
                res[s, here, LANES:] = out[:, LANES:].astype(jnp.bfloat16)

    def update(step, c):
        own_back = back[...]

        @pl.loop(0, chunk // LANES)
        def _(n):
            base = pl.multiple_of(c * chunk + n * LANES, LANES)
            here = pl.ds(base, LANES)
            cur[pl.ds(2 * plane + base, LANES)] = merged(
                codes[step, pl.ds(c * (chunk // LANES) + n, 1)], moved[here], ret[here], own_back)

    def halo_copies(step):
        two, one = 2 * plane, plane
        ahead_src = pick(nx * plane, 2 * plane)
        behind_src = pick(2 * plane, (nx + 1) * plane)
        return [
            pltpu.make_async_remote_copy(
                src_ref=cur.at[pl.ds(pl.multiple_of(ahead_src, plane), two)], dst_ref=halo.at[step, pl.ds(0, two)],
                send_sem=halo_send.at[0], recv_sem=halo_recv.at[step, 0],
                device_id={"space": ahead}, device_id_type=MESH),
            pltpu.make_async_remote_copy(
                src_ref=cur.at[pl.ds(pl.multiple_of(behind_src, plane), one)], dst_ref=halo.at[step, pl.ds(two, one)],
                send_sem=halo_send.at[1], recv_sem=halo_recv.at[step, 1],
                device_id={"space": behind}, device_id_type=MESH),
        ]

    def halo_place(step):
        two, one = 2 * plane, plane
        up_dst = pick(0, (nx + 2) * plane)
        down_dst = pick((nx + 2) * plane, plane)
        return [
            pltpu.make_async_copy(halo.at[step, pl.ds(0, two)], cur.at[pl.ds(pl.multiple_of(up_dst, plane), two)],
                                  local_sem.at[2, 0]),
            pltpu.make_async_copy(halo.at[step, pl.ds(two, one)], cur.at[pl.ds(pl.multiple_of(down_dst, plane), one)],
                                  local_sem.at[2, 1]),
        ]

    outs = []
    sent, back_sent = {}, {}
    waiting = set()

    def finish(step, c):
        for copy in back_sent[c]:
            copy.wait()
        update(step, c)
        waiting.discard(c)

    def send_rows(step, c):
        sent[c] = row_copies(c)
        for copy in sent[c]:
            copy.start()
        own_copy = row_local(c)
        own_copy.start()
        sent[c].append(own_copy)
        if step == STEPS - 1:
            outs.append(pltpu.make_async_copy(
                moved.at[pl.ds(c * chunk, chunk)], moved_out.at[pl.ds(c * chunk, chunk)], out_sem.at[0, c]))
            outs[-1].start()

    def collide_send(step, c):
        for copy in sent[c]:
            copy.wait()
        collide(step, c)
        back_sent[c] = res_copies(c)
        for copy in back_sent[c]:
            copy.start()
        own_copy = res_local(c)
        own_copy.start()
        back_sent[c].append(own_copy)

    edges = [0, CHUNKS - 1]
    order = list(range(1, CHUNKS - 1)) + edges
    later = list(range(2, CHUNKS - 2)) + [1, CHUNKS - 2] + edges
    for step in range(STEPS):
        if step == 0:
            for c in edges:
                loads[c].wait()
            halos = halo_copies(step)
            for copy in halos:
                copy.start()
            loaded = set(edges)
        else:
            halos = None
            order = later
        for n, c in enumerate(order):
            near = [k for k in (c - 1, c, c + 1) if 0 <= k < CHUNKS]
            if step == 0:
                for k in near:
                    if k not in loaded:
                        loads[k].wait()
                        loaded.add(k)
            else:
                if n == CHUNKS - 4:
                    near = sorted(waiting)
                for k in near:
                    if k in waiting:
                        finish(step - 1, k)
                if halos is None and not waiting.intersection(edges):
                    halos = halo_copies(step)
                    for copy in halos:
                        copy.start()
            if n == CHUNKS - 2:
                for copy in halos:
                    copy.wait()
                places = halo_place(step)
                for copy in places:
                    copy.start()
                for copy in places:
                    copy.wait()
            transport(c)
            send_rows(step, c)
            if step == 0 and n == 0:
                for copy in consts:
                    copy.wait()
            if n > 0:
                collide_send(step, order[n - 1])
        collide_send(step, order[-1])
        waiting = set(order)
    for c in order:
        for copy in back_sent[c]:
            copy.wait()
        outs.append(pltpu.make_async_copy(
            ret.at[pl.ds(c * chunk, chunk)], ret_out.at[pl.ds(c * chunk, chunk)], out_sem.at[1, c]))
        outs[-1].start()
    for copy in outs:
        copy.wait()


def final_kernel(codes, moved_ref, ret_ref, back_ref, out_ref):
    at = pl.program_id(0) * (out_ref.shape[0] // LANES)
    for n in range(out_ref.shape[0] // LANES):
        here = pl.ds(n * LANES, LANES)
        out_ref[here] = merged(codes[STEPS - 1, pl.ds(at + n, 1)], moved_ref[here], ret_ref[here], back_ref[...])


def body(dist, relax_rate, kinetic_cells, kinetic_count, map_a, map_b, map_c):
    nx, ny, nz, width = dist.shape
    groups = lax.axis_size("vel")
    slabs = lax.axis_size("space")
    cells = nx * ny * nz
    chunk = cells // CHUNKS
    rows = chunk // groups
    plane = ny * nz
    basis, back = tables()
    back = lax.dynamic_slice_in_dim(jnp.asarray(back), lax.axis_index("vel") * width, width, 1)
    back = jnp.pad(back, ((0, LANES - back.shape[0]), (0, 0))).astype(jnp.bfloat16)

    any_space = pl.BlockSpec(memory_space=pl.ANY)
    f32, bf16 = jnp.float32, jnp.bfloat16
    dims = (nx, ny, nz, width, groups, slabs)
    vmem = pl.BlockSpec(memory_space=pltpu.VMEM)
    moved, ret, codes = pl.pallas_call(
        functools.partial(kernel, dims),
        out_shape=(jax.ShapeDtypeStruct((cells, width), f32), jax.ShapeDtypeStruct((cells, width), bf16),
                   jax.ShapeDtypeStruct((STEPS, cells // LANES, LANES), f32)),
        in_specs=[pl.BlockSpec(memory_space=pltpu.SMEM)] + [vmem] * 4 + [any_space] * 4,
        out_specs=(any_space, any_space, vmem),
        scratch_shapes=[
            pltpu.VMEM(((nx + 4) * plane, width), f32),
            pltpu.VMEM((cells, width), f32),
            pltpu.VMEM((plane, width), f32),
            pltpu.VMEM((STEPS, 3 * plane, width), f32),
            pltpu.VMEM((cells, width), bf16),
            pltpu.VMEM((groups, CHUNKS * rows, width), bf16),
            pltpu.VMEM((groups, CHUNKS * rows, width), bf16),
            pltpu.VMEM((cells, width), bf16),
            pltpu.VMEM(map_a.shape, bf16),
            pltpu.VMEM(map_b.shape, bf16),
            pltpu.VMEM(map_c.shape, bf16),
            pltpu.VMEM((map_a.shape[0], LANES), bf16),
            pltpu.VMEM((LANES, LANES), f32),
            pltpu.SemaphoreType.DMA((CHUNKS,)),
            pltpu.SemaphoreType.DMA((3,)),
            pltpu.SemaphoreType.DMA((3, CHUNKS)),
            pltpu.SemaphoreType.DMA((2, CHUNKS)),
            pltpu.SemaphoreType.DMA((2,)),
            pltpu.SemaphoreType.DMA((STEPS, 2)),
            pltpu.SemaphoreType.DMA((CHUNKS, groups)),
            pltpu.SemaphoreType.DMA((CHUNKS, groups)),
            pltpu.SemaphoreType.DMA((CHUNKS, groups)),
            pltpu.SemaphoreType.DMA((CHUNKS, groups)),
        ],
        compiler_params=pltpu.CompilerParams(
            collective_id=0, has_side_effects=True, vmem_limit_bytes=67043328),
    )(kinetic_count, kinetic_cells, relax_rate.reshape(cells // LANES, LANES), jnp.asarray(basis), back,
      dist.reshape(cells, width), map_a, map_b, map_c)

    size = cells // 8
    out = pl.pallas_call(
        final_kernel,
        grid=(8,),
        out_shape=jax.ShapeDtypeStruct((cells, width), f32),
        in_specs=[
            pl.BlockSpec((STEPS, cells // LANES, LANES), lambda i: (0, 0, 0)),
            pl.BlockSpec((size, width), lambda i: (i, 0)),
            pl.BlockSpec((size, width), lambda i: (i, 0)),
            pl.BlockSpec((LANES, width), lambda i: (0, 0)),
        ],
        out_specs=pl.BlockSpec((size, width), lambda i: (i, 0)),
    )(codes, moved, ret, back)
    return out.reshape(dist.shape)


def solution(mesh):
    return jax.shard_map(
        body,
        mesh=mesh,
        in_specs=(
            P("space", None, None, "vel"),
            P("space", None, None),
            P(None, "space"),
            P(),
            P(),
            P(),
            P(),
        ),
        out_specs=P("space", None, None, "vel"),
        check_vma=False,
    )
```

profile of v0, /device:TPU:0, one launch (start us, length us, event | category | flops | bytes accessed | tf_op | source)
XLA Modules:
  0.0 128.8 jit_solution(7697240379929040125)
XLA Ops:
  0.0 0.7 dynamic-slice_convert_fusion
  0.7 1.6 %reshape.9.relax = f32[32,128]{1,0:T(8,128)} reshape(f32[16,16,16]{2,1,0:T(8,128)} %param.10) | data formatting | bytes 32768 | tf_op jit(solution)/shard_map/reshape | solution.py:434
  2.3 0.6 pad.5.back.back_ref
  2.9 118.1 %shard_map.91 = (f32[4096,256]{1,0:T(8,128)}, bf16[4096,256]{1,0:T(8,128)(2,1)}, f32[2,32,128]{2,1,0:T(8,128)}) custom-call(s32[2,4]{1,0:T(2,128)} %counts.1, s32[2,4096]{1,0:T(2,128)} %kin_cells.1, f32[32,128]{1,0:T(8,128)} %reshape.9.relax, f32[24,2048]{1,0:T(8,128)} %constant.18.clone.basis_rows, bf16[128,256]{1,0:T(8,128)(2,1)} %pad.5.back.back_ref, ...), custom_call_target="tpu_custom_call" | custom-call | tf_op jit(solution)/shard_map/pallas_call | solution.py:401
  121.0 7.8 %shard_map.92 = f32[4096,256]{1,0:T(8,128)} custom-call(f32[2,32,128]{2,1,0:T(8,128)} %get-tuple-element.8.codes, f32[4096,256]{1,0:T(8,128)} %get-tuple-element.9.moved_ref, bf16[4096,256]{1,0:T(8,128)(2,1)} %get-tuple-element.10.ret_ref, bf16[128,256]{1,0:T(8,128)(2,1)} %pad.5.back.back_ref), custom_call_target="tpu_custom_call" | custom-call | tf_op jit(solution)/shard_map/pallas_call | solution.py:438
where the time goes:
time: 129 us
  Pallas kernels  126 us (98%)
  local copies, waits for them, and re-layouts  2.94 us (2%)
    pallas_call x1, Pallas kernels, body(): pl.pallas_call(functools.partial(kernel, dims), out_shape=(jax.ShapeDtype...  118 us
    pallas_call x1, Pallas kernels, body(): pl.pallas_call(final_kernel, grid=(8,), out_shape=jax.ShapeDtypeStruct((c...  7.78 us

commit v1 on v0

--- a/solution.py
+++ b/solution.py
@@ -17,7 +17,8 @@
 SPACING = 0.5
 COLLIDE = 0.5
 LANES = 128
-CHUNKS = 8
+CHUNKS = 4
+LAG = 1
 MESH = pl.DeviceIdType.MESH
 
 
@@ -105,29 +106,6 @@
     pl.semaphore_signal(barrier, inc=1, device_id={"space": behind}, device_id_type=MESH)
     pl.semaphore_wait(barrier, groups + 1)
 
-    @pl.loop(0, basis.shape[0] // LANES)
-    def _(n):
-        here = pl.ds(pl.multiple_of(n * LANES, LANES), LANES)
-        part = basis_rows[:, here]
-        whole = jnp.concatenate([part, jnp.zeros((LANES - part.shape[0], LANES), jnp.float32)], axis=0)
-        basis[here] = whole.T.astype(jnp.bfloat16)
-
-    groups_of = cells // LANES
-    span = 4 * LANES
-    for step in range(STEPS):
-        count = counts[step, slab]
-        flags = jnp.zeros((groups_of, LANES), jnp.float32)
-        for n in range(cells // span):
-            which = kin_cells[step:step + 1, n * span:(n + 1) * span]
-            live = n * span + lax.broadcasted_iota(jnp.int32, (1, span), 1) < count
-            quotient = jnp.where(live, lax.div(which, LANES), -1)
-            hot_high = lax.broadcasted_iota(jnp.int32, (groups_of, span), 0) == quotient
-            hot_low = lax.broadcasted_iota(jnp.int32, (LANES, span), 0) == lax.rem(which, LANES)
-            flags += lax.dot_general(
-                jnp.where(hot_high, 1.0, 0.0).astype(jnp.bfloat16), jnp.where(hot_low, 1.0, 0.0).astype(jnp.bfloat16),
-                (((1,), (1,)), ((), ())), preferred_element_type=jnp.float32)
-        codes[step] = jnp.where(flags > 0.5, -COLLIDE, relax[...])
-
     lane = lax.broadcasted_iota(jnp.int32, (1, LANES), 1)
     vy = (((lane // GZ) % GY).astype(jnp.float32) - 0.5 * (GY - 1)) * SPACING
     vz = ((lane % GZ).astype(jnp.float32) - 0.5 * (GZ - 1)) * SPACING
@@ -193,6 +171,30 @@
                     result = mid - total
                     moved[at(index - 2, y), cols] = result
                     sendbuf[at(index - 2, y), cols] = result.astype(jnp.bfloat16)
+
+    def prepare():
+        @pl.loop(0, basis.shape[0] // LANES)
+        def _(n):
+            here = pl.ds(pl.multiple_of(n * LANES, LANES), LANES)
+            part = basis_rows[:, here]
+            whole = jnp.concatenate([part, jnp.zeros((LANES - part.shape[0], LANES), jnp.float32)], axis=0)
+            basis[here] = whole.T.astype(jnp.bfloat16)
+
+        groups_of = cells // LANES
+        span = 4 * LANES
+        for step in range(STEPS):
+            count = counts[step, slab]
+            flags = jnp.zeros((groups_of, LANES), jnp.float32)
+            for n in range(cells // span):
+                which = kin_cells[step:step + 1, n * span:(n + 1) * span]
+                live = n * span + lax.broadcasted_iota(jnp.int32, (1, span), 1) < count
+                quotient = jnp.where(live, lax.div(which, LANES), -1)
+                hot_high = lax.broadcasted_iota(jnp.int32, (groups_of, span), 0) == quotient
+                hot_low = lax.broadcasted_iota(jnp.int32, (LANES, span), 0) == lax.rem(which, LANES)
+                flags += lax.dot_general(
+                    jnp.where(hot_high, 1.0, 0.0).astype(jnp.bfloat16), jnp.where(hot_low, 1.0, 0.0).astype(jnp.bfloat16),
+                    (((1,), (1,)), ((), ())), preferred_element_type=jnp.float32)
+            codes[step] = jnp.where(flags > 0.5, -COLLIDE, relax[...])
 
     def row_copies(c):
         out = []
@@ -331,6 +333,7 @@
         else:
             halos = None
             order = later
+        queue = []
         for n, c in enumerate(order):
             near = [k for k in (c - 1, c, c + 1) if 0 <= k < CHUNKS]
             if step == 0:
@@ -339,7 +342,7 @@
                         loads[k].wait()
                         loaded.add(k)
             else:
-                if n == CHUNKS - 4:
+                if n == max(CHUNKS - 4, 1):
                     near = sorted(waiting)
                 for k in near:
                     if k in waiting:
@@ -359,11 +362,14 @@
             transport(c)
             send_rows(step, c)
             if step == 0 and n == 0:
+                prepare()
                 for copy in consts:
                     copy.wait()
-            if n > 0:
-                collide_send(step, order[n - 1])
-        collide_send(step, order[-1])
+            queue.append(c)
+            if len(queue) > LAG:
+                collide_send(step, queue.pop(0))
+        while queue:
+            collide_send(step, queue.pop(0))
         waiting = set(order)
     for c in order:
         for copy in back_sent[c]:

time: 129 us -> 125 us (0.969)
  Pallas kernels: 126 us -> 122 us
    pallas_call x1, Pallas kernels: 118 us -> 114 us  [body(): pl.pallas_call(functools.partial(kernel, dims), out_shape=(jax.ShapeDtype...]
where the time goes in v1:
time: 125 us; the launch traced here: 124 us
  Pallas kernels  122 us (98%)
  local copies, waits for them, and re-layouts  2.94 us (2%)
    pallas_call x1, Pallas kernels, body(): pl.pallas_call(functools.partial(kernel, dims), out_shape=(jax.ShapeDtype...  114 us
    pallas_call x1, Pallas kernels, body(): pl.pallas_call(final_kernel, grid=(8,), out_shape=jax.ShapeDtypeStruct((c...  7.78 us

profile of v1, /device:TPU:0, one launch (start us, length us, event | category | flops | bytes accessed | tf_op | source)
XLA Modules:
  0.0 124.5 jit_solution(8659194713108708557)
XLA Ops:
  0.0 0.7 dynamic-slice_convert_fusion
  0.7 1.6 %reshape.9.relax = f32[32,128]{1,0:T(8,128)} reshape(f32[16,16,16]{2,1,0:T(8,128)} %param.10) | data formatting | bytes 32768 | tf_op jit(solution)/shard_map/reshape | solution.py:440
  2.3 0.6 pad.5.back.back_ref
  2.9 113.8 %shard_map.91 = (f32[4096,256]{1,0:T(8,128)}, bf16[4096,256]{1,0:T(8,128)(2,1)}, f32[2,32,128]{2,1,0:T(8,128)}) custom-call(s32[2,4]{1,0:T(2,128)} %counts.1, s32[2,4096]{1,0:T(2,128)} %kin_cells.1, f32[32,128]{1,0:T(8,128)} %reshape.9.relax, f32[24,2048]{1,0:T(8,128)} %constant.18.clone.basis_rows, bf16[128,256]{1,0:T(8,128)(2,1)} %pad.5.back.back_ref, ...), custom_call_target="tpu_custom_call" | custom-call | tf_op jit(solution)/shard_map/pallas_call | solution.py:407
  116.7 7.8 %shard_map.92 = f32[4096,256]{1,0:T(8,128)} custom-call(f32[2,32,128]{2,1,0:T(8,128)} %get-tuple-element.8.codes, f32[4096,256]{1,0:T(8,128)} %get-tuple-element.9.moved_ref, bf16[4096,256]{1,0:T(8,128)(2,1)} %get-tuple-element.10.ret_ref, bf16[128,256]{1,0:T(8,128)(2,1)} %pad.5.back.back_ref), custom_call_target="tpu_custom_call" | custom-call | tf_op jit(solution)/shard_map/pallas_call | solution.py:444
